TPU v7x, 32 devices: a whole 2x2x4 slice. The times are simulated.
32 devices in a mesh: fits: 2 (over y), tm: 4 (over z), space: 4 (over x, core).
Axes of the slice: x: 2, y: 2, z: 4, core: 2. Of those that a mesh axis runs over, the one named last changes fastest.
Arguments:
- coupling: float32 [16, 4, 384, 384], P(('fits', 'tm'), 'space'), parts along dimension 0, may hold values from -0.034701105 to 1.0347011, as said below
- schur_inverse: float32 [16, 4, 384, 384], P(('fits', 'tm'), 'space'), parts along dimension 0, may hold values from -0.052051657 to 1.0720517, as said below
- entry_rows: int32 [16, 4, 2048], P(('fits', 'tm'), 'space'), parts along dimension 0, may hold values from 0 to 383
- entry_shift: int32 [16, 4, 2048], P(('fits', 'tm'), 'space'), parts along dimension 0, may hold values from -3 to 3
- entry_hyper: int32 [16, 4, 2048], P(('fits', 'tm'), 'space'), parts along dimension 0, may hold values from 0 to 3
- entry_values: float32 [16, 4, 2048], P(('fits', 'tm'), 'space'), parts along dimension 0, may hold values from -0.3125 to 0.3125
Outputs:
- marginal_cov: float32 [16, 4, 384, 384], P(('fits', 'tm'), 'space'), parts along dimension 0
- gradient: float32 [8], P('fits'), parts along dimension 0
There are 2 independent parts, one for each index of `fits`. A program takes and returns all parts, laid end to end along the dimension named above; each array names one. Nothing has to cross between parts.
Inputs may be any that keep to these rules, and one draw needn't show every extreme that they name: Every block of coupling has entries within the stated range. Every block of schur_inverse is symmetric positive definite.
All inputs are finite; a program needn't handle non-finite values.
Results may differ from a plain program's by a relative error of at most 0.0001.
Values sent between devices are 32-bit elements; how exact they have to be, the bound alone decides.
A program may use at most 128 MiB of HBM per device.

v0:
```python
import jax
import jax.numpy as jnp
from jax import lax
from jax.sharding import PartitionSpec as P

NHYP = 4


def prefix(shard, axis, combine, identity):
    devices, mine = (lax.axis_size(axis), lax.axis_index(axis))
    everything = jax.tree.map(lambda part: lax.all_gather(part, axis), shard)
    start = jax.tree.map(
        lambda part, zero: jnp.broadcast_to(jnp.asarray(zero, part.dtype), part.shape),
        shard,
        identity,
    )

    def step(k, before):
        at = devices - 1 - k
        reached = at > mine
        new = combine(before, jax.tree.map(lambda part: part[at], everything))
        return jax.tree.map(lambda a, b: jnp.where(reached, a, b), new, before)

    return lax.fori_loop(0, devices, step, start)


def apply_map(coupling, schur_inverse, current):
    product = jnp.einsum("sij,sjk->sik", coupling, current, precision=lax.Precision.HIGHEST)
    return (
        jnp.einsum("sik,slk->sil", product, coupling, precision=lax.Precision.HIGHEST)
        + schur_inverse
    )


def combine_maps(earlier, later):
    joined_g = jnp.einsum("sij,sjk->sik", later[0], earlier[0], precision=lax.Precision.HIGHEST)
    joined_s = apply_map(later[0], later[1], earlier[1])
    return (joined_g, joined_s)


def on_device(coupling, schur_inverse, entry_rows, entry_shift, entry_hyper, entry_values):
    time_count = coupling.shape[0]
    order = coupling.shape[2]
    composite_g = coupling[time_count - 1]
    composite_s = schur_inverse[time_count - 1]
    position = 0
    composite_s = apply_map(coupling[position], schur_inverse[position], composite_s)
    composite_g = jnp.einsum(
        "sij,sjk->sik", coupling[position], composite_g, precision=lax.Precision.HIGHEST
    )
    identity = (
        jnp.broadcast_to(jnp.eye(order, dtype=jnp.float32), composite_g.shape),
        jnp.zeros_like(composite_s),
    )
    scanned = prefix((composite_g, composite_s), "tm", combine_maps, identity)
    boundary = scanned[1]
    results = [None] * time_count
    current = boundary
    for position in range(time_count - 1, -1, -1):
        current = apply_map(coupling[position], schur_inverse[position], current)
        results[position] = current
    marginal_cov = jnp.stack(results, axis=0)
    columns = jnp.mod(entry_rows + entry_shift, order)
    flat_index = entry_rows * order + columns
    flattened = marginal_cov.reshape(time_count, coupling.shape[1], order * order)
    picked = jnp.take_along_axis(flattened, flat_index, axis=2)
    one_hot = (entry_hyper[..., None] == jnp.arange(NHYP, dtype=jnp.int32)).astype(jnp.float32)
    local_terms = -0.5 * jnp.sum((entry_values * picked)[..., None] * one_hot, axis=(0, 1, 2))
    gradient = lax.psum(local_terms, ("tm", "space"))
    return (marginal_cov, gradient)


def solution(mesh):
    in_specs = (
        P(("fits", "tm"), "space", None, None),
        P(("fits", "tm"), "space", None, None),
        P(("fits", "tm"), "space", None),
        P(("fits", "tm"), "space", None),
        P(("fits", "tm"), "space", None),
        P(("fits", "tm"), "space", None),
    )
    out_specs = (P(("fits", "tm"), "space", None, None), P("fits"))
    return jax.shard_map(
        on_device, mesh=mesh, in_specs=in_specs, out_specs=out_specs, check_vma=False
    )
```

profile of v0, /device:TPU:0, one launch (start us, length us, event | category | flops | bytes accessed | tf_op | source)
XLA Modules:
  0.0 225.0 jit_solution(2873054929532404826)
XLA Ops:
  7.2 0.0 all-gather.7.cloned.1.call-start
  7.2 2.6 %fusion.16 = f32[384,384]{1,0:T(8,128)S(1)} fusion(f32[2,1,384,384]{3,2,1,0:T(8,128)} %param.9, f32[2,1,384,384]{3,2,1,0:T(8,128)} %param.8), kind=kOutput, calls=%fused_computation.23 | convolution fusion | flops 679477248 | bytes 1769472 | tf_op jit(solution)/shard_map/sij,sjk->sik/dot_general | solution.py:28
  9.8 3.1 %convolution_add_fusion.3 = f32[384,384]{1,0:T(8,128)} fusion(f32[384,384]{1,0:T(8,128)S(1)} %fusion.16, f32[2,1,384,384]{3,2,1,0:T(8,128)} %param.9, f32[2,1,384,384]{3,2,1,0:T(8,128)S(1)} %copy-done), kind=kOutput, calls=%fused_computation.18 | convolution fusion | flops 679624704 | bytes 2359296 | tf_op jit(solution)/shard_map/sik,slk->sil/dot_general | solution.py:30
  13.0 0.0 all-gather.7.cloned.1.call-update
  13.0 0.0 all-gather.5.cloned.1.call-start
  13.1 2.1 fusion.20
  15.2 0.0 all-gather.5.cloned.1.call-update
  15.2 0.6 copy.23
  15.8 0.7 bitcast_or_fusion
  16.5 49.3 %all-gather.7.cloned.1.call-done = f32[1536,384]{1,0:T(8,128)} async-done(((f32[384,384]{1,0:T(8,128)}), f32[1536,384]{1,0:T(8,128)}) %all-gather.7.cloned.1.call-update) | async-done | bytes 2359312 | tf_op jit(solution)/shard_map/all_gather | solution.py:11
  65.9 50.9 %all-gather.5.cloned.1.call-done = f32[1536,384]{1,0:T(8,128)} async-done(((f32[384,384]{1,0:T(8,128)}), f32[1536,384]{1,0:T(8,128)}) %all-gather.5.cloned.1.call-update) | async-done | bytes 2359312 | tf_op jit(solution)/shard_map/all_gather | solution.py:11
  116.8 19.9 %while.16 = (s32[]{:T(128)}, f32[1,384,384]{2,1,0:T(8,128)S(1)}, s32[]{:T(128)}, f32[4,1,384,384]{3,2,1,0:T(8,128)}, f32[4,1,384,384]{3,2,1,0:T(8,128)}, /*index=5*/s32[]{:T(128)}, s32[]{:T(128)}, s32[]{:T(128)}, s32[]{:T(128)}) while((s32[]{:T(128)}, f32[1,384,384]{2,1,0:T(8,128)S(1)}, s32[]{:T(128)}, ...), condition=%wide.region_1.2_spmd.clone, body=%wide.region_0.1_spmd.clone.sunk | while | flops 1359544320 | bytes 4720802 | solution.py:24
  116.8 2.3 %fusion.54 = f32[384,384]{1,0:T(8,128)S(1)} fusion(f32[1,384,384]{2,1,0:T(8,128)S(1)} %get-tuple-element.221, f32[4,1,384,384]{3,2,1,0:T(8,128)} %get-tuple-element.232, s32[]{:T(128)S(6)} %select_n.74, pred[]{:T(512)S(6)} %compare.3), kind=kOutput, calls=%fused_computation.4.clone.1 | convolution fusion | flops 679624704 | bytes 1769477 | tf_op jit(solution)/shard_map/while/body/eval_jaxpr/sij,sjk->sik/dot_general | solution.py:28
  119.1 2.6 %fusion.55 = f32[1,384,384]{2,1,0:T(8,128)S(1)} fusion(f32[384,384]{1,0:T(8,128)S(1)} %fusion.54, f32[4,1,384,384]{3,2,1,0:T(8,128)} %get-tuple-element.233, s32[]{:T(128)S(6)} %select_n.74, f32[1,384,384]{2,1,0:T(8,128)S(1)} %get-tuple-element.221, f32[4,1,384,384]{3,2,1,0:T(8,128)} %get-tuple-element.232, pred[]{:T(512)S(6)} %compare.3, pred[]{:T(512)S(6)} %gt.12), kind=kOutput, calls=%fused_computation.3.clone.1 | convolution fusion | flops 679919616 | bytes 2951168 | tf_op jit(solution)/shard_map/while/body/eval_jaxpr/sik,slk->sil/dot_general | solution.py:30
  121.8 2.3 %fusion.54 = f32[384,384]{1,0:T(8,128)S(1)} fusion(f32[1,384,384]{2,1,0:T(8,128)S(1)} %get-tuple-element.221, f32[4,1,384,384]{3,2,1,0:T(8,128)} %get-tuple-element.232, s32[]{:T(128)S(6)} %select_n.74, pred[]{:T(512)S(6)} %compare.3), kind=kOutput, calls=%fused_computation.4.clone.1 | convolution fusion | flops 679624704 | bytes 1769477 | tf_op jit(solution)/shard_map/while/body/eval_jaxpr/sij,sjk->sik/dot_general | solution.py:28
  124.1 2.6 %fusion.55 = f32[1,384,384]{2,1,0:T(8,128)S(1)} fusion(f32[384,384]{1,0:T(8,128)S(1)} %fusion.54, f32[4,1,384,384]{3,2,1,0:T(8,128)} %get-tuple-element.233, s32[]{:T(128)S(6)} %select_n.74, f32[1,384,384]{2,1,0:T(8,128)S(1)} %get-tuple-element.221, f32[4,1,384,384]{3,2,1,0:T(8,128)} %get-tuple-element.232, pred[]{:T(512)S(6)} %compare.3, pred[]{:T(512)S(6)} %gt.12), kind=kOutput, calls=%fused_computation.3.clone.1 | convolution fusion | flops 679919616 | bytes 2951168 | tf_op jit(solution)/shard_map/while/body/eval_jaxpr/sik,slk->sil/dot_general | solution.py:30
  126.7 2.3 %fusion.54 = f32[384,384]{1,0:T(8,128)S(1)} fusion(f32[1,384,384]{2,1,0:T(8,128)S(1)} %get-tuple-element.221, f32[4,1,384,384]{3,2,1,0:T(8,128)} %get-tuple-element.232, s32[]{:T(128)S(6)} %select_n.74, pred[]{:T(512)S(6)} %compare.3), kind=kOutput, calls=%fused_computation.4.clone.1 | convolution fusion | flops 679624704 | bytes 1769477 | tf_op jit(solution)/shard_map/while/body/eval_jaxpr/sij,sjk->sik/dot_general | solution.py:28
  129.1 2.6 %fusion.55 = f32[1,384,384]{2,1,0:T(8,128)S(1)} fusion(f32[384,384]{1,0:T(8,128)S(1)} %fusion.54, f32[4,1,384,384]{3,2,1,0:T(8,128)} %get-tuple-element.233, s32[]{:T(128)S(6)} %select_n.74, f32[1,384,384]{2,1,0:T(8,128)S(1)} %get-tuple-element.221, f32[4,1,384,384]{3,2,1,0:T(8,128)} %get-tuple-element.232, pred[]{:T(512)S(6)} %compare.3, pred[]{:T(512)S(6)} %gt.12), kind=kOutput, calls=%fused_computation.3.clone.1 | convolution fusion | flops 679919616 | bytes 2951168 | tf_op jit(solution)/shard_map/while/body/eval_jaxpr/sik,slk->sil/dot_general | solution.py:30
  131.7 2.3 %fusion.54 = f32[384,384]{1,0:T(8,128)S(1)} fusion(f32[1,384,384]{2,1,0:T(8,128)S(1)} %get-tuple-element.221, f32[4,1,384,384]{3,2,1,0:T(8,128)} %get-tuple-element.232, s32[]{:T(128)S(6)} %select_n.74, pred[]{:T(512)S(6)} %compare.3), kind=kOutput, calls=%fused_computation.4.clone.1 | convolution fusion | flops 679624704 | bytes 1769477 | tf_op jit(solution)/shard_map/while/body/eval_jaxpr/sij,sjk->sik/dot_general | solution.py:28
  134.1 2.6 %fusion.55 = f32[1,384,384]{2,1,0:T(8,128)S(1)} fusion(f32[384,384]{1,0:T(8,128)S(1)} %fusion.54, f32[4,1,384,384]{3,2,1,0:T(8,128)} %get-tuple-element.233, s32[]{:T(128)S(6)} %select_n.74, f32[1,384,384]{2,1,0:T(8,128)S(1)} %get-tuple-element.221, f32[4,1,384,384]{3,2,1,0:T(8,128)} %get-tuple-element.232, pred[]{:T(512)S(6)} %compare.3, pred[]{:T(512)S(6)} %gt.12), kind=kOutput, calls=%fused_computation.3.clone.1 | convolution fusion | flops 679919616 | bytes 2951168 | tf_op jit(solution)/shard_map/while/body/eval_jaxpr/sik,slk->sil/dot_general | solution.py:30
  136.7 2.0 fusion.14
  138.8 2.0 convolution_add_fusion.2
  140.8 2.9 %fusion.23 = f32[384,384]{1,0:T(8,128)} fusion(f32[384,384]{1,0:T(8,128)S(1)} %convolution_add_fusion.2, f32[2,1,384,384]{3,2,1,0:T(8,128)S(1)} %copy-done), kind=kOutput, calls=%fused_computation.30 | convolution fusion | flops 679477248 | bytes 1769472 | tf_op jit(solution)/shard_map/sij,sjk->sik/dot_general | solution.py:28
  143.7 1.4 stack.19
  145.1 3.1 %convolution_add_fusion.1 = f32[384,384]{1,0:T(8,128)S(1)} fusion(f32[384,384]{1,0:T(8,128)} %fusion.23, f32[2,1,384,384]{3,2,1,0:T(8,128)S(1)} %copy-done.1, f32[2,1,384,384]{3,2,1,0:T(8,128)S(1)} %copy-done), kind=kOutput, calls=%fused_computation.16 | convolution fusion | flops 679624704 | bytes 2359296 | tf_op jit(solution)/shard_map/sik,slk->sil/dot_general | solution.py:30
  148.2 0.6 stack.18
  148.8 0.5 copy-done.2
  149.2 1.1 maximum_bitcast_fusion
  150.4 34.9 %gather_fusion = f32[4096]{0:T(1024)S(1)} fusion(f32[2,147456]{1,0:T(2,128)S(1)} %maximum_bitcast_fusion, s32[4096]{0:T(1024)S(1)} %bitcast.81), kind=kCustom, calls=%fused_computation | custom fusion | bytes 65536 | tf_op jit(solution)/shard_map/jit(take_along_axis)/gather | solution.py:66
  185.4 0.1 select_reduce_fusion
  185.5 31.6 %psum.7 = f32[4]{0:T(128)} all-reduce(f32[4]{0:T(128)S(1)} %broadcast_multiply_fusion), channel_id=1, replica_groups=mesh['fits'=2,'tm'=4,'space'=4] {'tm','space'}, use_global_device_ids=true, to_apply=%region_3.4 | all-reduce | flops 4 | bytes 32 | tf_op jit(solution)/shard_map/psum | solution.py:69
  217.1 1.1 pad_maximum_fusion
  (21 shorter events, 0.1 us)
Async XLA Ops:
  7.2 2.7 %copy-start = (f32[2,1,384,384]{3,2,1,0:T(8,128)S(1)}, f32[2,1,384,384]{3,2,1,0:T(8,128)}, u32[]{:S(2)}) copy-start(f32[2,1,384,384]{3,2,1,0:T(8,128)} %param.8) | copy-start | bytes 3538948
  7.2 58.7 %all-gather.7.cloned.1.call-start = ((), (), s32[]{:S(2)}) async-start(), calls=%async_computation.1 | async-start | bytes 2949120 | tf_op jit(solution)/shard_map/all_gather | solution.py:11
  13.0 2.2 copy-start.5
  13.0 2.8 %copy-start.6 = (s32[2,1,2048]{2,1,0:T(1,128)S(1)}, s32[2,1,2048]{2,1,0:T(1,128)}, u32[]{:S(2)}) copy-start(s32[2,1,2048]{2,1,0:T(1,128)} %param.10) | copy-start | bytes 49156
  13.0 2.8 %copy-start.7 = (s32[2,1,2048]{2,1,0:T(1,128)S(1)}, s32[2,1,2048]{2,1,0:T(1,128)}, u32[]{:S(2)}) copy-start(s32[2,1,2048]{2,1,0:T(1,128)} %param.11) | copy-start | bytes 49156
  13.0 103.7 %all-gather.5.cloned.1.call-start = ((), (), s32[]{:S(2)}) async-start(), calls=%async_computation | async-start | bytes 2949120 | tf_op jit(solution)/shard_map/all_gather | solution.py:11
  136.7 2.1 copy-start.1
  148.2 1.1 copy-start.2
  150.4 35.0 %copy-start.4 = (s32[2,1,2048]{2,1,0:T(1,128)S(1)}, s32[2,1,2048]{2,1,0:T(1,128)}, u32[]{:S(2)}) copy-start(s32[2,1,2048]{2,1,0:T(1,128)} %get-tuple-element.179) | copy-start | bytes 49156
  150.4 35.0 %copy-start.8 = (f32[2,1,2048]{2,1,0:T(1,128)S(1)}, f32[2,1,2048]{2,1,0:T(1,128)}, u32[]{:S(2)}) copy-start(f32[2,1,2048]{2,1,0:T(1,128)} %param.13) | copy-start | bytes 49156
  150.4 35.0 %copy-start.3 = (s32[2,1,2048]{2,0,1:T(2,128)S(1)}, s32[2,1,2048]{2,0,1:T(2,128)}, u32[]{:S(2)}) copy-start(s32[2,1,2048]{2,0,1:T(2,128)} %copy.23) | copy-start | bytes 49156
Sparse Core Ops, SparseCore 0:
  13.1 52.6 all-gather.6
  68.0 48.7 all-gather.4
where the time goes:
time: 226 us; the launch traced here: 225 us
  waiting for transfers between devices  100 us (44%)
  local copies, waits for them, and re-layouts  38 us (17%)
  matrix products  37.6 us (17%)
  blocking collectives  31.6 us (14%)
  between operations  14.3 us (6%)
  other arithmetic  3.1 us (1%)
    all_gather x2, waiting for transfers between devices, prefix(): everything = jax.tree.map(lambda part: lax.all_gather(part, axis), shard)  100 us
    gather x1, local copies, waits for them, and re-layouts, on_device(): picked = jnp.take_along_axis(flattened, flat_index, axis=2)  34.9 us
    psum x1, blocking collectives, on_device(): gradient = lax.psum(local_terms, ('tm', 'space'))  31.6 us
    dot_general x7, matrix products, apply_map(): jnp.einsum('sik,slk->sil', product, coupling, precision=lax.Precision.HIG...  18.8 us
    dot_general x7, matrix products, apply_map(): jnp.einsum('sij,sjk->sik', coupling, current, precision=lax.Precision.HIG...  16.8 us
  transfers between devices with their start and end apart: 2, of which 2 were waited for; matrix products, arithmetic and copies ran while one was open for 2% of the time, Pallas kernels for 0%

commit v1 on v0

--- a/solution.py
+++ b/solution.py
@@ -66,7 +66,9 @@
     picked = jnp.take_along_axis(flattened, flat_index, axis=2)
     one_hot = (entry_hyper[..., None] == jnp.arange(NHYP, dtype=jnp.int32)).astype(jnp.float32)
     local_terms = -0.5 * jnp.sum((entry_values * picked)[..., None] * one_hot, axis=(0, 1, 2))
-    gradient = lax.psum(local_terms, ("tm", "space"))
+    gradient = local_terms
+    for over in ("space", "tm"):
+        gradient = lax.psum(gradient, over)
     return (marginal_cov, gradient)
 
 

time: 226 us -> 211 us (0.934)
  blocking collectives: 31.6 us -> 16.8 us
    psum x1 -> x2, blocking collectives: 31.6 us -> 16.8 us  [on_device(): gradient = lax.psum(gradient, over)]
where the time goes in v1:
time: 211 us; the launch traced here: 210 us
  waiting for transfers between devices  100 us (47%)
  local copies, waits for them, and re-layouts  38 us (18%)
  matrix products  37.6 us (18%)
  blocking collectives  16.8 us (8%)
  between operations  14.3 us (7%)
  other arithmetic  3.09 us (1%)
    all_gather x2, waiting for transfers between devices, prefix(): everything = jax.tree.map(lambda part: lax.all_gather(part, axis), shard)  100 us
    gather x1, local copies, waits for them, and re-layouts, on_device(): picked = jnp.take_along_axis(flattened, flat_index, axis=2)  34.9 us
    dot_general x7, matrix products, apply_map(): jnp.einsum('sik,slk->sil', product, coupling, precision=lax.Precision.HIG...  18.8 us
    psum x2, blocking collectives, on_device(): gradient = lax.psum(gradient, over)  16.8 us
    dot_general x7, matrix products, apply_map(): jnp.einsum('sij,sjk->sik', coupling, current, precision=lax.Precision.HIG...  16.8 us
  transfers between devices with their start and end apart: 2, of which 2 were waited for; matrix products, arithmetic and copies ran while one was open for 2% of the time, Pallas kernels for 0%

profile of v1, /device:TPU:0, one launch (start us, length us, event | category | flops | bytes accessed | tf_op | source)
XLA Modules:
  0.0 210.3 jit_solution(7050171508525071041)
XLA Ops:
  7.2 0.0 all-gather.7.cloned.1.call-start
  7.2 2.6 %fusion.16 = f32[384,384]{1,0:T(8,128)S(1)} fusion(f32[2,1,384,384]{3,2,1,0:T(8,128)} %param.9, f32[2,1,384,384]{3,2,1,0:T(8,128)} %param.8), kind=kOutput, calls=%fused_computation.23 | convolution fusion | flops 679477248 | bytes 1769472 | tf_op jit(solution)/shard_map/sij,sjk->sik/dot_general | solution.py:28
  9.8 3.2 %convolution_add_fusion.3 = f32[384,384]{1,0:T(8,128)} fusion(f32[384,384]{1,0:T(8,128)S(1)} %fusion.16, f32[2,1,384,384]{3,2,1,0:T(8,128)} %param.9, f32[2,1,384,384]{3,2,1,0:T(8,128)S(1)} %copy-done), kind=kOutput, calls=%fused_computation.18 | convolution fusion | flops 679624704 | bytes 2359296 | tf_op jit(solution)/shard_map/sik,slk->sil/dot_general | solution.py:30
  13.0 0.0 all-gather.7.cloned.1.call-update
  13.0 0.0 all-gather.5.cloned.1.call-start
  13.1 2.1 fusion.20
  15.2 0.6 copy.23
  15.8 0.7 bitcast_or_fusion
  16.5 49.3 %all-gather.7.cloned.1.call-done = f32[1536,384]{1,0:T(8,128)} async-done(((f32[384,384]{1,0:T(8,128)}), f32[1536,384]{1,0:T(8,128)}) %all-gather.7.cloned.1.call-update) | async-done | bytes 2359312 | tf_op jit(solution)/shard_map/all_gather | solution.py:11
  65.9 50.9 %all-gather.5.cloned.1.call-done = f32[1536,384]{1,0:T(8,128)} async-done(((f32[384,384]{1,0:T(8,128)}), f32[1536,384]{1,0:T(8,128)}) %all-gather.5.cloned.1.call-update) | async-done | bytes 2359312 | tf_op jit(solution)/shard_map/all_gather | solution.py:11
  116.8 19.9 %while.16 = (s32[]{:T(128)}, f32[1,384,384]{2,1,0:T(8,128)S(1)}, s32[]{:T(128)}, f32[4,1,384,384]{3,2,1,0:T(8,128)}, f32[4,1,384,384]{3,2,1,0:T(8,128)}, /*index=5*/s32[]{:T(128)}, s32[]{:T(128)}, s32[]{:T(128)}, s32[]{:T(128)}) while((s32[]{:T(128)}, f32[1,384,384]{2,1,0:T(8,128)S(1)}, s32[]{:T(128)}, ...), condition=%wide.region_1.2_spmd.clone, body=%wide.region_0.1_spmd.clone.sunk | while | flops 1359544320 | bytes 4720802 | solution.py:24
  116.8 2.3 %fusion.54 = f32[384,384]{1,0:T(8,128)S(1)} fusion(f32[1,384,384]{2,1,0:T(8,128)S(1)} %get-tuple-element.221, f32[4,1,384,384]{3,2,1,0:T(8,128)} %get-tuple-element.232, s32[]{:T(128)S(6)} %select_n.74, pred[]{:T(512)S(6)} %compare.3), kind=kOutput, calls=%fused_computation.4.clone.1 | convolution fusion | flops 679624704 | bytes 1769477 | tf_op jit(solution)/shard_map/while/body/eval_jaxpr/sij,sjk->sik/dot_general | solution.py:28
  119.1 2.6 %fusion.55 = f32[1,384,384]{2,1,0:T(8,128)S(1)} fusion(f32[384,384]{1,0:T(8,128)S(1)} %fusion.54, f32[4,1,384,384]{3,2,1,0:T(8,128)} %get-tuple-element.233, s32[]{:T(128)S(6)} %select_n.74, f32[1,384,384]{2,1,0:T(8,128)S(1)} %get-tuple-element.221, f32[4,1,384,384]{3,2,1,0:T(8,128)} %get-tuple-element.232, pred[]{:T(512)S(6)} %compare.3, pred[]{:T(512)S(6)} %gt.12), kind=kOutput, calls=%fused_computation.3.clone.1 | convolution fusion | flops 679919616 | bytes 2951168 | tf_op jit(solution)/shard_map/while/body/eval_jaxpr/sik,slk->sil/dot_general | solution.py:30
  121.8 2.3 %fusion.54 = f32[384,384]{1,0:T(8,128)S(1)} fusion(f32[1,384,384]{2,1,0:T(8,128)S(1)} %get-tuple-element.221, f32[4,1,384,384]{3,2,1,0:T(8,128)} %get-tuple-element.232, s32[]{:T(128)S(6)} %select_n.74, pred[]{:T(512)S(6)} %compare.3), kind=kOutput, calls=%fused_computation.4.clone.1 | convolution fusion | flops 679624704 | bytes 1769477 | tf_op jit(solution)/shard_map/while/body/eval_jaxpr/sij,sjk->sik/dot_general | solution.py:28
  124.1 2.6 %fusion.55 = f32[1,384,384]{2,1,0:T(8,128)S(1)} fusion(f32[384,384]{1,0:T(8,128)S(1)} %fusion.54, f32[4,1,384,384]{3,2,1,0:T(8,128)} %get-tuple-element.233, s32[]{:T(128)S(6)} %select_n.74, f32[1,384,384]{2,1,0:T(8,128)S(1)} %get-tuple-element.221, f32[4,1,384,384]{3,2,1,0:T(8,128)} %get-tuple-element.232, pred[]{:T(512)S(6)} %compare.3, pred[]{:T(512)S(6)} %gt.12), kind=kOutput, calls=%fused_computation.3.clone.1 | convolution fusion | flops 679919616 | bytes 2951168 | tf_op jit(solution)/shard_map/while/body/eval_jaxpr/sik,slk->sil/dot_general | solution.py:30
  126.8 2.3 %fusion.54 = f32[384,384]{1,0:T(8,128)S(1)} fusion(f32[1,384,384]{2,1,0:T(8,128)S(1)} %get-tuple-element.221, f32[4,1,384,384]{3,2,1,0:T(8,128)} %get-tuple-element.232, s32[]{:T(128)S(6)} %select_n.74, pred[]{:T(512)S(6)} %compare.3), kind=kOutput, calls=%fused_computation.4.clone.1 | convolution fusion | flops 679624704 | bytes 1769477 | tf_op jit(solution)/shard_map/while/body/eval_jaxpr/sij,sjk->sik/dot_general | solution.py:28
  129.1 2.6 %fusion.55 = f32[1,384,384]{2,1,0:T(8,128)S(1)} fusion(f32[384,384]{1,0:T(8,128)S(1)} %fusion.54, f32[4,1,384,384]{3,2,1,0:T(8,128)} %get-tuple-element.233, s32[]{:T(128)S(6)} %select_n.74, f32[1,384,384]{2,1,0:T(8,128)S(1)} %get-tuple-element.221, f32[4,1,384,384]{3,2,1,0:T(8,128)} %get-tuple-element.232, pred[]{:T(512)S(6)} %compare.3, pred[]{:T(512)S(6)} %gt.12), kind=kOutput, calls=%fused_computation.3.clone.1 | convolution fusion | flops 679919616 | bytes 2951168 | tf_op jit(solution)/shard_map/while/body/eval_jaxpr/sik,slk->sil/dot_general | solution.py:30
  131.7 2.3 %fusion.54 = f32[384,384]{1,0:T(8,128)S(1)} fusion(f32[1,384,384]{2,1,0:T(8,128)S(1)} %get-tuple-element.221, f32[4,1,384,384]{3,2,1,0:T(8,128)} %get-tuple-element.232, s32[]{:T(128)S(6)} %select_n.74, pred[]{:T(512)S(6)} %compare.3), kind=kOutput, calls=%fused_computation.4.clone.1 | convolution fusion | flops 679624704 | bytes 1769477 | tf_op jit(solution)/shard_map/while/body/eval_jaxpr/sij,sjk->sik/dot_general | solution.py:28
  134.1 2.6 %fusion.55 = f32[1,384,384]{2,1,0:T(8,128)S(1)} fusion(f32[384,384]{1,0:T(8,128)S(1)} %fusion.54, f32[4,1,384,384]{3,2,1,0:T(8,128)} %get-tuple-element.233, s32[]{:T(128)S(6)} %select_n.74, f32[1,384,384]{2,1,0:T(8,128)S(1)} %get-tuple-element.221, f32[4,1,384,384]{3,2,1,0:T(8,128)} %get-tuple-element.232, pred[]{:T(512)S(6)} %compare.3, pred[]{:T(512)S(6)} %gt.12), kind=kOutput, calls=%fused_computation.3.clone.1 | convolution fusion | flops 679919616 | bytes 2951168 | tf_op jit(solution)/shard_map/while/body/eval_jaxpr/sik,slk->sil/dot_general | solution.py:30
  136.7 2.0 fusion.14
  138.8 2.0 convolution_add_fusion.2
  140.8 2.9 %fusion.23 = f32[384,384]{1,0:T(8,128)} fusion(f32[384,384]{1,0:T(8,128)S(1)} %convolution_add_fusion.2, f32[2,1,384,384]{3,2,1,0:T(8,128)S(1)} %copy-done), kind=kOutput, calls=%fused_computation.30 | convolution fusion | flops 679477248 | bytes 1769472 | tf_op jit(solution)/shard_map/sij,sjk->sik/dot_general | solution.py:28
  143.7 1.4 stack.19
  145.1 3.1 %convolution_add_fusion.1 = f32[384,384]{1,0:T(8,128)S(1)} fusion(f32[384,384]{1,0:T(8,128)} %fusion.23, f32[2,1,384,384]{3,2,1,0:T(8,128)S(1)} %copy-done.1, f32[2,1,384,384]{3,2,1,0:T(8,128)S(1)} %copy-done), kind=kOutput, calls=%fused_computation.16 | convolution fusion | flops 679624704 | bytes 2359296 | tf_op jit(solution)/shard_map/sik,slk->sil/dot_general | solution.py:30
  148.2 0.6 stack.18
  148.8 0.5 copy-done.2
  149.3 1.1 maximum_bitcast_fusion
  150.4 34.9 %gather_fusion = f32[4096]{0:T(1024)S(1)} fusion(f32[2,147456]{1,0:T(2,128)S(1)} %maximum_bitcast_fusion, s32[4096]{0:T(1024)S(1)} %bitcast.81), kind=kCustom, calls=%fused_computation | custom fusion | bytes 65536 | tf_op jit(solution)/shard_map/jit(take_along_axis)/gather | solution.py:66
  185.4 0.1 select_reduce_fusion
  185.6 6.4 %psum.14 = f32[4]{0:T(128)S(1)} all-reduce(f32[4]{0:T(128)S(1)} %broadcast_multiply_fusion), channel_id=1, replica_groups=mesh['fits'=2,'tm'=4,'space'=4] {'space'}, use_global_device_ids=true, to_apply=%region_3.4 | all-reduce | flops 4 | bytes 32 | tf_op jit(solution)/shard_map/psum | solution.py:71
  192.0 10.4 %psum.15 = f32[4]{0:T(128)} all-reduce(f32[4]{0:T(128)S(1)} %psum.14), channel_id=1, replica_groups=mesh['fits'=2,'tm'=4,'space'=4] {'tm'}, use_global_device_ids=true, to_apply=%region_4.5 | all-reduce | flops 4 | bytes 32 | tf_op jit(solution)/shard_map/psum | solution.py:71
  202.4 1.1 pad_maximum_fusion
  (22 shorter events, 0.1 us)
Async XLA Ops:
  7.2 2.7 %copy-start = (f32[2,1,384,384]{3,2,1,0:T(8,128)S(1)}, f32[2,1,384,384]{3,2,1,0:T(8,128)}, u32[]{:S(2)}) copy-start(f32[2,1,384,384]{3,2,1,0:T(8,128)} %param.8) | copy-start | bytes 3538948
  7.2 58.7 %all-gather.7.cloned.1.call-start = ((), (), s32[]{:S(2)}) async-start(), calls=%async_computation.1 | async-start | bytes 2949120 | tf_op jit(solution)/shard_map/all_gather | solution.py:11
  13.0 2.2 %copy-start.5 = (s32[2,1,2048]{2,1,0:T(1,128)S(1)}, s32[2,1,2048]{2,1,0:T(1,128)}, u32[]{:S(2)}) copy-start(s32[2,1,2048]{2,1,0:T(1,128)} %param.12) | copy-start | bytes 49156
  13.0 2.8 %copy-start.6 = (s32[2,1,2048]{2,1,0:T(1,128)S(1)}, s32[2,1,2048]{2,1,0:T(1,128)}, u32[]{:S(2)}) copy-start(s32[2,1,2048]{2,1,0:T(1,128)} %param.10) | copy-start | bytes 49156
  13.0 2.8 %copy-start.7 = (s32[2,1,2048]{2,1,0:T(1,128)S(1)}, s32[2,1,2048]{2,1,0:T(1,128)}, u32[]{:S(2)}) copy-start(s32[2,1,2048]{2,1,0:T(1,128)} %param.11) | copy-start | bytes 49156
  13.0 103.7 %all-gather.5.cloned.1.call-start = ((), (), s32[]{:S(2)}) async-start(), calls=%async_computation | async-start | bytes 2949120 | tf_op jit(solution)/shard_map/all_gather | solution.py:11
  136.7 2.1 copy-start.1
  148.2 1.1 copy-start.2
  150.4 35.0 %copy-start.4 = (s32[2,1,2048]{2,1,0:T(1,128)S(1)}, s32[2,1,2048]{2,1,0:T(1,128)}, u32[]{:S(2)}) copy-start(s32[2,1,2048]{2,1,0:T(1,128)} %get-tuple-element.179) | copy-start | bytes 49156
  150.4 35.0 %copy-start.8 = (f32[2,1,2048]{2,1,0:T(1,128)S(1)}, f32[2,1,2048]{2,1,0:T(1,128)}, u32[]{:S(2)}) copy-start(f32[2,1,2048]{2,1,0:T(1,128)} %param.13) | copy-start | bytes 49156
  150.4 35.0 %copy-start.3 = (s32[2,1,2048]{2,0,1:T(2,128)S(1)}, s32[2,1,2048]{2,0,1:T(2,128)}, u32[]{:S(2)}) copy-start(s32[2,1,2048]{2,0,1:T(2,128)} %copy.23) | copy-start | bytes 49156
Sparse Core Ops, SparseCore 0:
  13.1 52.6 all-gather.6
  68.0 48.7 all-gather.4
